TPU v7x, 32 devices: a whole 2x2x4 slice. The times are simulated.
32 devices in a mesh: seq: 16 (over z, y, core), tp: 2 (over x).
Axes of the slice: x: 2, y: 2, z: 4, core: 2. Of those that a mesh axis runs over, the one named last changes fastest.
Arguments:
- queries: bfloat16 [8192, 2048], P('seq', 'tp'), may hold values from -9 to 9
- keys: bfloat16 [8192, 2048], P('seq', 'tp'), may hold values from -9 to 9
- values: bfloat16 [8192, 2048], P('seq', 'tp'), may hold values from -6 to 6
- residual: bfloat16 [8192, 2048], P(('seq', 'tp')), may hold values from -36 to 36
- out_weight: bfloat16 [2048, 2048], P('tp'), may hold values from -0.125 to 0.125
- norm_gain: float32 [2048], replicated, may hold values from 0.25 to 1.75
- router: bfloat16 [2048, 8], replicated, may hold values from -0.25 to 0.25
- gate_weight: bfloat16 [2048, 5504], P('seq', 'tp'), may hold values from -0.125 to 0.125
- up_weight: bfloat16 [2048, 5504], P('seq', 'tp'), may hold values from -0.125 to 0.125
- down_weight: bfloat16 [5504, 2048], P('tp', 'seq'), may hold values from -0.078125 to 0.078125
- gate_shrink: bfloat16 [2048, 128], replicated, may hold values from -0.125 to 0.125
- up_shrink: bfloat16 [2048, 128], replicated, may hold values from -0.125 to 0.125
- gate_widen_maps: bfloat16 [128, 5504], P(None, 'tp'), may hold values from -0.75 to 0.75
- upward_widen_maps: bfloat16 [128, 5504], P(None, 'tp'), may hold values from -0.75 to 0.75
- down_shrink: bfloat16 [5504, 128], P('tp'), may hold values from -0.078125 to 0.078125
- down_expand: bfloat16 [128, 2048], replicated, may hold values from -1.5 to 1.5
- routing: int32 [8192, 2], P('seq'), may hold values from 0 to 7, all different within a row
- doc_lengths: int32 [4], replicated, may hold values from 1 to 4096, 8192 in all
Outputs:
- output: bfloat16 [8192, 2048], P(('seq', 'tp'))
Inputs may be any that keep to these rules, and one draw needn't show every extreme that they name: `routing`: each row names two different experts. `doc_lengths`: the lengths sum to 8192.
All inputs are finite; a program needn't handle non-finite values.
Results may differ from a plain program's by a relative error of at most 0.015.
Values may be sent and summed in bfloat16 or wider, within the bound.
A program may use at most 128 MiB of HBM per device.

v0:
```python
import math
import jax
import jax.numpy as jnp
from jax import lax
from jax.sharding import PartitionSpec as P

HEAD = 128
EXPERTS = 8
RANK = 16
WINDOW = 4096
adapter_scale_factor = 2.0
epsilon = 1e-05
masked_score = -1e30


def from_behind(value, axis, steps):
    count = lax.axis_size(axis)
    initial, last = (max(0, -steps), min(count, count - steps))
    return lax.ppermute(value, axis, [(source, source + steps) for source in range(initial, last)])


def document_of(positions, doc_ends):
    return jnp.sum((positions[:, None] >= doc_ends[None, :]).astype(jnp.int32), axis=1)


def on_device(
    queries,
    keys,
    values,
    residual,
    out_weight,
    norm_gain,
    router,
    gate_weight,
    up_weight,
    down_weight,
    gate_shrink,
    up_shrink,
    gate_widen_maps,
    upward_widen_maps,
    down_shrink,
    down_expand,
    routing,
    doc_lengths,
):
    tokens_here = queries.shape[0]
    total_width = queries.shape[1]
    heads_here = total_width // HEAD
    reach_blocks = WINDOW // tokens_here
    seq_index = lax.axis_index("seq")
    stacked = jnp.stack((keys, values))
    held_blocks = from_behind(stacked, "seq", 1)
    for section_index in range(reach_blocks.bit_length() - 1):
        earlier = from_behind(held_blocks, "seq", 1 << section_index)
        held_blocks = jnp.concatenate((earlier, held_blocks), axis=1)
    window = jnp.concatenate((held_blocks, stacked), axis=1)
    key_count = window.shape[1]
    doc_ends = jnp.cumsum(doc_lengths)
    query_positions = seq_index * tokens_here + jnp.arange(tokens_here, dtype=jnp.int32)
    key_positions = (seq_index - reach_blocks) * tokens_here + jnp.arange(
        key_count, dtype=jnp.int32
    )
    visible = key_positions[None, :] <= query_positions[:, None]
    visible = visible & (query_positions[:, None] - key_positions[None, :] < WINDOW)
    visible = visible & (key_positions[None, :] >= 0)
    visible = visible & (
        document_of(query_positions, doc_ends)[:, None]
        == document_of(key_positions, doc_ends)[None, :]
    )
    score_scale = 1.0 / math.sqrt(HEAD)
    query_heads = queries.reshape(tokens_here, heads_here, HEAD).transpose(1, 0, 2)
    key_heads = window[0].reshape(key_count, heads_here, HEAD).transpose(1, 0, 2)
    value_heads = window[1].reshape(key_count, heads_here, HEAD).transpose(1, 0, 2)

    def one_head(operands):
        query_one, key_one, value_one = operands
        scores = (
            jnp.einsum("qd,kd->qk", query_one, key_one, preferred_element_type=jnp.float32)
            * score_scale
        )
        scores = jnp.where(visible, scores, masked_score)
        largest = jnp.max(scores, axis=1, keepdims=True)
        exponent = jnp.exp(scores - largest)
        attn_weights = (exponent / jnp.sum(exponent, axis=1, keepdims=True)).astype(jnp.bfloat16)
        return jnp.dot(attn_weights, value_one, preferred_element_type=jnp.float32).astype(
            jnp.bfloat16
        )

    attended = lax.map(one_head, (query_heads, key_heads, value_heads))
    attended = attended.transpose(1, 0, 2).reshape(tokens_here, total_width)
    projected = lax.psum_scatter(
        jnp.dot(attended, out_weight, preferred_element_type=jnp.float32),
        "tp",
        scatter_dimension=0,
        tiled=True,
    )
    after_attention_state = residual.astype(jnp.float32) + projected
    mean_square = jnp.mean(after_attention_state * after_attention_state, axis=1, keepdims=True)
    normed_own = (after_attention_state * lax.rsqrt(mean_square + epsilon) * norm_gain).astype(
        jnp.bfloat16
    )
    normed = lax.all_gather(normed_own, "tp", axis=0, tiled=True)
    rank_gate = jnp.dot(normed, gate_shrink, preferred_element_type=jnp.float32).astype(
        jnp.bfloat16
    )
    rank_up = jnp.dot(normed, up_shrink, preferred_element_type=jnp.float32).astype(jnp.bfloat16)
    logits = jnp.dot(normed, router, preferred_element_type=jnp.float32)
    expert_ids = jnp.arange(EXPERTS, dtype=jnp.int32)
    first_logit = jnp.sum(jnp.where(routing[:, 0:1] == expert_ids[None, :], logits, 0.0), axis=1)
    second_logit = jnp.sum(jnp.where(routing[:, 1:2] == expert_ids[None, :], logits, 0.0), axis=1)
    weight_first = jax.nn.sigmoid(first_logit - second_logit)[:, None]
    weight_second = jax.nn.sigmoid(second_logit - first_logit)[:, None]
    frozen_gate_output = jnp.dot(
        normed,
        lax.all_gather(gate_weight, "seq", axis=0, tiled=True),
        preferred_element_type=jnp.float32,
    )
    frozen_up_output = jnp.dot(
        normed,
        lax.all_gather(up_weight, "seq", axis=0, tiled=True),
        preferred_element_type=jnp.float32,
    )
    column_expert = jnp.arange(EXPERTS * RANK, dtype=jnp.int32) // RANK
    hiddens = []
    pickers = []
    for slot_index in range(2):
        picker = column_expert[None, :] == routing[:, slot_index : slot_index + 1]
        pickers.append(picker)
        selected_gate_widen = jnp.where(picker, rank_gate, jnp.zeros_like(rank_gate))
        selected_upward_widen = jnp.where(picker, rank_up, jnp.zeros_like(rank_up))
        gate_complete_output = frozen_gate_output + adapter_scale_factor * jnp.dot(
            selected_gate_widen, gate_widen_maps, preferred_element_type=jnp.float32
        )
        upward_complete_output = frozen_up_output + adapter_scale_factor * jnp.dot(
            selected_upward_widen, upward_widen_maps, preferred_element_type=jnp.float32
        )
        hiddens.append(jax.nn.silu(gate_complete_output) * upward_complete_output)
    mixture = (weight_first * hiddens[0] + weight_second * hiddens[1]).astype(jnp.bfloat16)
    shrunk_first = jnp.dot(
        hiddens[0].astype(jnp.bfloat16), down_shrink, preferred_element_type=jnp.float32
    )
    shrunk_second = jnp.dot(
        hiddens[1].astype(jnp.bfloat16), down_shrink, preferred_element_type=jnp.float32
    )
    rank_down = weight_first * jnp.where(pickers[0], shrunk_first, 0.0) + weight_second * jnp.where(
        pickers[1], shrunk_second, 0.0
    )
    downward_adapter_term = jnp.dot(
        mixture,
        lax.all_gather(down_weight, "seq", axis=1, tiled=True),
        preferred_element_type=jnp.float32,
    )
    downward_token_rows, rank_rows = (
        lax.psum_scatter(
            downward_adapter_term.astype(jnp.bfloat16), "tp", scatter_dimension=0, tiled=True
        ).astype(jnp.float32),
        lax.psum_scatter(
            rank_down.astype(jnp.bfloat16), "tp", scatter_dimension=0, tiled=True
        ).astype(jnp.float32),
    )
    low_rank_product = jnp.dot(
        rank_rows.astype(jnp.bfloat16), down_expand, preferred_element_type=jnp.float32
    )
    return (
        after_attention_state + downward_token_rows + adapter_scale_factor * low_rank_product
    ).astype(jnp.bfloat16)


def solution(mesh):
    placed = (
        P("seq", "tp"),
        P("seq", "tp"),
        P("seq", "tp"),
        P(("seq", "tp"), None),
        P("tp", None),
        P(),
        P(),
        P("seq", "tp"),
        P("seq", "tp"),
        P("tp", "seq"),
        P(),
        P(),
        P(None, "tp"),
        P(None, "tp"),
        P("tp", None),
        P(),
        P("seq", None),
        P(),
    )
    return jax.shard_map(
        on_device, mesh=mesh, in_specs=placed, out_specs=P(("seq", "tp"), None), check_vma=False
    )
```

profile of v0, /device:TPU:0, one launch (start us, length us, event | category | flops | bytes accessed | tf_op | source)
XLA Modules:
  0.0 907.2 jit_solution(18371292692780234825)
XLA Ops:
  6.5 1.6 copy.27
  8.1 1.9 copy.28
  11.2 2.5 collective-permute-start
  13.7 3.6 collective-permute-done
  17.4 23.8 %collective-permute-start.1 = (bf16[2,512,1024]{1,2,0:T(8,128)(2,1)S(1)}, bf16[2,512,1024]{1,2,0:T(8,128)(2,1)S(1)}, u32[]{:S(2)}, u32[]{:S(2)}) collective-permute-start(bf16[2,512,1024]{1,2,0:T(8,128)(2,1)S(1)} %collective-permute-done), channel_id=1, source_target_pairs={{0,2},{2,4},{4,6},{6,8},{8,10},{10,12},{12,14},{14,16},{16,18},{18... | collective-permute-start | bytes 6291464 | tf_op jit(solution)/shard_map/ppermute | solution.py:19
  41.2 3.6 collective-permute-done.1
  45.5 26.3 %collective-permute-start.2 = (bf16[2,1024,1024]{1,2,0:T(8,128)(2,1)S(1)}, bf16[2,1024,1024]{1,2,0:T(8,128)(2,1)S(1)}, u32[]{:S(2)}, u32[]{:S(2)}) collective-permute-start(bf16[2,1024,1024]{1,2,0:T(8,128)(2,1)S(1)} %pad_maximum_fusion.1), channel_id=1, source_target_pairs={{0,4},{2,6},{4,8},{6,10},{8,12},{10,14},{12,16},{14,18},{16,20},{1... | collective-permute-start | bytes 12582920 | tf_op jit(solution)/shard_map/ppermute | solution.py:19
  71.9 89.8 %collective-permute-done.2 = bf16[2,1024,1024]{1,2,0:T(8,128)(2,1)S(1)} collective-permute-done((bf16[2,1024,1024]{1,2,0:T(8,128)(2,1)S(1)}, bf16[2,1024,1024]{1,2,0:T(8,128)(2,1)S(1)}, u32[]{:S(2)}, u32[]{:S(2)}) %collective-permute-start.2) | collective-permute-done | bytes 4194336 | tf_op jit(solution)/shard_map/ppermute | solution.py:19
  161.6 4.5 pad_maximum_fusion
  166.2 7.8 collective-permute-start.3
  174.0 2.3 copy.26
  176.7 172.0 %collective-permute-done.3 = bf16[2,2048,1024]{1,2,0:T(8,128)(2,1)} collective-permute-done((bf16[2,2048,1024]{1,2,0:T(8,128)(2,1)}, bf16[2,2048,1024]{1,2,0:T(8,128)(2,1)}, u32[]{:S(2)}, u32[]{:S(2)}) %collective-permute-start.3) | collective-permute-done | bytes 8388640 | tf_op jit(solution)/shard_map/ppermute | solution.py:19
  348.7 8.3 constant_dynamic-update-slice_fusion.5
  357.1 4.8 constant_dynamic-update-slice_fusion.4
  361.9 1.5 constant_dynamic-update-slice_fusion.3
  363.4 1.5 constant_dynamic-update-slice_fusion.2
  364.9 1.5 constant_dynamic-update-slice_fusion.1
  366.5 14.5 %fusion.66 = (bf16[1,4608,1024]{1,2,0:T(8,128)(2,1)}, bf16[1,4608,1024]{1,2,0:T(8,128)(2,1)}) fusion(bf16[2,4608,1024]{1,2,0:T(8,128)(2,1)} %constant_dynamic-update-slice_fusion.1), kind=kLoop, calls=%fused_computation.92 | loop fusion | bytes 37748736 | tf_op jit(solution)/shard_map/slice | solution.py:73
  380.9 81.6 %while.11 = (s32[]{:T(128)}, bf16[8,512,128]{1,2,0:T(8,128)(2,1)S(1)}, bf16[8,512,128]{1,2,0:T(8,128)(2,1)}, bf16[8,4608,128]{1,2,0:T(8,128)(2,1)}, bf16[8,4608,...) while((s32[]{:T(128)}, ...), condition=%wide.region_6.7_spmd.clone, body=%wide.region_3.6_spmd.clone.sunk | while | flops 1243413504 | bytes 31514736 | solution.py:89
  380.9 5.7 fusion.97
  386.6 1.4 fusion.98
  388.1 2.9 fusion.99
  391.1 5.7 fusion.97
  396.8 1.4 fusion.98
  398.2 2.9 fusion.99
  401.3 5.7 fusion.97
  407.0 1.4 fusion.98
  408.4 2.9 fusion.99
  411.5 5.7 fusion.97
  417.2 1.4 fusion.98
  418.6 2.9 fusion.99
  421.6 5.7 fusion.97
  427.4 1.4 fusion.98
  428.8 2.9 fusion.99
  431.8 5.7 fusion.97
  437.6 1.4 fusion.98
  439.0 2.9 fusion.99
  442.0 5.7 fusion.97
  449.1 2.9 fusion.99
  452.2 5.7 fusion.97
  459.3 2.9 fusion.99
  462.6 6.6 fusion.68
  469.3 56.5 %reduce-scatter.4.cloned.1.call-done = f32[256,2048]{1,0:T(8,128)} async-done(((f32[512,2048]{1,0:T(8,128)}), f32[256,2048]{1,0:T(8,128)}) %reduce-scatter.4.cloned.1.call-update) | async-done | bytes 2097168 | tf_op jit(solution)/shard_map/reduce_scatter | solution.py:91
  525.9 1.9 multiply_reduce_fusion
  527.8 2.9 multiply_convert_fusion
  532.8 31.3 %all-gather.5.cloned.1.call-done = bf16[512,2048]{1,0:T(8,128)(2,1)} async-done(((bf16[256,2048]{1,0:T(8,128)(2,1)}), bf16[512,2048]{1,0:T(8,128)(2,1)}) %all-gather.5.cloned.1.call-update) | async-done | bytes 2097168 | tf_op jit(solution)/shard_map/all_gather | solution.py:102
  564.1 2.3 select_reduce_fusion
  566.3 2.3 convolution_convert_fusion.2
  568.7 2.3 convolution_convert_fusion.1
  571.0 3.4 fusion.48
  574.4 3.4 fusion.47
  577.8 83.8 %all-gather.7.cloned.1.call-done = bf16[2048,2752]{0,1:T(8,128)(2,1)} async-done(((bf16[128,2752]{0,1:T(8,128)(2,1)}), bf16[2048,2752]{0,1:T(8,128)(2,1)}) %all-gather.7.cloned.1.call-update) | async-done | bytes 11272208 | tf_op jit(solution)/shard_map/all_gather | solution.py:115
  661.5 10.4 %fusion.69 = f32[512,2752]{0,1:T(8,128)} fusion(bf16[512,2048]{1,0:T(8,128)(2,1)S(1)} %copy-done.3, bf16[2048,2752]{0,1:T(8,128)(2,1)} %all-gather.7.cloned.1.call-done), kind=kOutput, calls=%fused_computation.95 | convolution fusion | flops 5771362304 | bytes 19005440 | tf_op jit(solution)/shard_map/dot_general | solution.py:113
  671.9 85.1 %all-gather.9.cloned.1.call-done = bf16[2048,2752]{0,1:T(8,128)(2,1)} async-done(((bf16[128,2752]{0,1:T(8,128)(2,1)}), bf16[2048,2752]{0,1:T(8,128)(2,1)}) %all-gather.9.cloned.1.call-update) | async-done | bytes 11272208 | tf_op jit(solution)/shard_map/all_gather | solution.py:120
  757.0 10.6 %fusion.70 = f32[512,2752]{0,1:T(8,128)} fusion(bf16[512,2048]{1,0:T(8,128)(2,1)S(1)} %copy-done.3, bf16[2048,2752]{0,1:T(8,128)(2,1)} %all-gather.9.cloned.1.call-done), kind=kOutput, calls=%fused_computation.96 | convolution fusion | flops 5771362304 | bytes 19005440 | tf_op jit(solution)/shard_map/dot_general | solution.py:118
  767.6 4.5 add_multiply_fusion.1
  773.1 3.6 copy-done.25
  776.7 2.1 add_multiply_fusion
  778.9 2.4 copy-done.2
  781.3 1.6 fusion.44
  783.1 69.4 %all-gather.11.cloned.1.call-done = bf16[2752,2048]{1,0:T(8,128)(2,1)} async-done(((bf16[2752,128]{1,0:T(8,128)(2,1)}), bf16[2752,2048]{1,0:T(8,128)(2,1)}) %all-gather.11.cloned.1.call-update) | async-done | bytes 11272208 | tf_op jit(solution)/shard_map/all_gather | solution.py:150
  852.5 13.2 %convolution_convert_fusion = bf16[512,2048]{1,0:T(8,128)(2,1)} fusion(bf16[2752,2048]{1,0:T(8,128)(2,1)} %all-gather.11.cloned.1.call-done, f32[512,2752]{0,1:T(8,128)} %copy-done.2, f32[512,2752]{0,1:T(8,128)} %copy-done.1, f32[512]{0:T(512)S(1)} %get-tuple-element.111, f32[512]{0:T(512)S(1)} %get-tuple-element.112), kind=kOutput, calls=%fused_computation.26 | convolution fusion | flops 5778046976 | bytes 24645632 | tf_op jit(solution)/shard_map/dot_general | solution.py:148
  865.8 31.5 %reduce-scatter.6.cloned.1.call-done = bf16[256,2048]{1,0:T(8,128)(2,1)} async-done(((bf16[512,2048]{1,0:T(8,128)(2,1)}), bf16[256,2048]{1,0:T(8,128)(2,1)}) %reduce-scatter.6.cloned.1.call-update) | async-done | bytes 1048592 | tf_op jit(solution)/shard_map/reduce_scatter | solution.py:154
  897.3 3.1 fusion.28
  (102 shorter events, 9.2 us)
Async XLA Ops:
  6.5 564.4 %copy-start = (bf16[128,2752]{0,1:T(8,128)(2,1)S(1)}, bf16[128,2752]{0,1:T(8,128)(2,1)}, u32[]{:S(2)}) copy-start(bf16[128,2752]{0,1:T(8,128)(2,1)} %param.32) | copy-start | bytes 2113540
  6.5 519.3 %reduce-scatter.4.cloned.1.call-start = ((), (), s32[]{:S(2)}) async-start(), calls=%async_computation.3 | async-start | bytes 6291456 | tf_op jit(solution)/shard_map/reduce_scatter | solution.py:91
  8.1 1.9 copy-start.9
  10.0 1.0 copy-start.11
  11.2 6.2 collective-permute-start
  17.4 27.5 %collective-permute-start.1 = (bf16[2,512,1024]{1,2,0:T(8,128)(2,1)S(1)}, bf16[2,512,1024]{1,2,0:T(8,128)(2,1)S(1)}, u32[]{:S(2)}, u32[]{:S(2)}) collective-permute-start(bf16[2,512,1024]{1,2,0:T(8,128)(2,1)S(1)} %collective-permute-done), channel_id=1, source_target_pairs={{0,2},{2,4},{4,6},{6,8},{8,10},{10,12},{12,14},{14,16},{16,18},{18... | collective-permute-start | bytes 6291464 | tf_op jit(solution)/shard_map/ppermute | solution.py:19
  44.8 121.3 %copy-start.5 = (bf16[2,512,1024]{1,2,0:T(8,128)(2,1)}, bf16[2,512,1024]{1,2,0:T(8,128)(2,1)S(1)}, u32[]{:S(2)}) copy-start(bf16[2,512,1024]{1,2,0:T(8,128)(2,1)S(1)} %collective-permute-done.1) | copy-start | bytes 6291460
  45.5 130.8 %copy-start.23 = (s32[4]{0:T(128)S(1)}, s32[4]{0:T(128)}, u32[]{:S(2)}) copy-start(s32[4]{0:T(128)} %param.37) | copy-start | bytes 52
  45.5 116.1 %collective-permute-start.2 = (bf16[2,1024,1024]{1,2,0:T(8,128)(2,1)S(1)}, bf16[2,1024,1024]{1,2,0:T(8,128)(2,1)S(1)}, u32[]{:S(2)}, u32[]{:S(2)}) collective-permute-start(bf16[2,1024,1024]{1,2,0:T(8,128)(2,1)S(1)} %pad_maximum_fusion.1), channel_id=1, source_target_pairs={{0,4},{2,6},{4,8},{6,10},{8,12},{10,14},{12,16},{14,18},{16,20},{1... | collective-permute-start | bytes 12582920 | tf_op jit(solution)/shard_map/ppermute | solution.py:19
  161.6 4.5 copy-start.7
  166.2 182.6 %collective-permute-start.3 = (bf16[2,2048,1024]{1,2,0:T(8,128)(2,1)}, bf16[2,2048,1024]{1,2,0:T(8,128)(2,1)}, u32[]{:S(2)}, u32[]{:S(2)}) collective-permute-start(bf16[2,2048,1024]{1,2,0:T(8,128)(2,1)} %pad_maximum_fusion), channel_id=1, source_target_pairs={{0,8},{2,10},{4,12},{6,14},{8,16},{10,18},{12,20},{14,22},{16,24},... | collective-permute-start | bytes 25165832 | tf_op jit(solution)/shard_map/ppermute | solution.py:19
  357.1 4.8 copy-start.6
  361.9 3.0 copy-start.10
  361.9 3.0 copy-start.12
  366.5 14.5 %copy-start.15 = (bf16[8,512,128]{1,2,0:T(8,128)(2,1)S(1)}, bf16[8,512,128]{1,2,0:T(8,128)(2,1)}, u32[]{:S(2)}) copy-start(bf16[8,512,128]{1,2,0:T(8,128)(2,1)} %custom-call.1) | copy-start | bytes 3145732
  462.6 63.3 %copy-start.8 = (bf16[256,2048]{1,0:T(8,128)(2,1)S(1)}, bf16[256,2048]{1,0:T(8,128)(2,1)}, u32[]{:S(2)}) copy-start(bf16[256,2048]{1,0:T(8,128)(2,1)} %param.23) | copy-start | bytes 3145732
  469.2 58.6 %copy-start.20 = (f32[2048]{0:T(1024)S(1)}, f32[2048]{0:T(1024)}, u32[]{:S(2)}) copy-start(f32[2048]{0:T(1024)} %param.25) | copy-start | bytes 24580
  469.2 63.5 %copy-start.21 = (s32[512,2]{0,1:T(2,128)S(1)}, s32[512,2]{0,1:T(2,128)}, u32[]{:S(2)}) copy-start(s32[512,2]{0,1:T(2,128)} %param.36) | copy-start | bytes 12292
  469.2 94.8 %copy-start.19 = (bf16[2048,8]{0,1:T(8,128)(2,1)S(1)}, bf16[2048,8]{0,1:T(8,128)(2,1)}, u32[]{:S(2)}) copy-start(bf16[2048,8]{0,1:T(8,128)(2,1)} %param.26) | copy-start | bytes 98308
  469.2 97.1 %copy-start.17 = (bf16[2048,128]{1,0:T(8,128)(2,1)S(1)}, bf16[2048,128]{1,0:T(8,128)(2,1)}, u32[]{:S(2)}) copy-start(bf16[2048,128]{1,0:T(8,128)(2,1)} %param.30) | copy-start | bytes 1572868
  469.2 94.8 %all-gather.5.cloned.1.call-start = ((), (), s32[]{:S(2)}) async-start(), calls=%async_computation.4 | async-start | bytes 3145728 | tf_op jit(solution)/shard_map/all_gather | solution.py:102
  527.8 40.8 %copy-start.18 = (bf16[2048,128]{1,0:T(8,128)(2,1)S(1)}, bf16[2048,128]{1,0:T(8,128)(2,1)}, u32[]{:S(2)}) copy-start(bf16[2048,128]{1,0:T(8,128)(2,1)} %param.31) | copy-start | bytes 1572868
  530.8 130.7 %all-gather.7.cloned.1.call-start = ((), (), s32[]{:S(2)}) async-start(), calls=%async_computation.5 | async-start | bytes 11976704 | tf_op jit(solution)/shard_map/all_gather | solution.py:115
  531.5 225.5 %all-gather.9.cloned.1.call-start = ((), (), s32[]{:S(2)}) async-start(), calls=%async_computation.6 | async-start | bytes 11976704 | tf_op jit(solution)/shard_map/all_gather | solution.py:120
  532.1 320.4 %all-gather.11.cloned.1.call-start = ((), (), s32[]{:S(2)}) async-start(), calls=%async_computation.7 | async-start | bytes 11976704 | tf_op jit(solution)/shard_map/all_gather | solution.py:150
  532.7 333.1 %reduce-scatter.8.cloned.1.call-start = ((), (), s32[]{:S(2)}) async-start(), calls=%async_computation.9 | async-start | bytes 196608 | tf_op jit(solution)/shard_map/reduce_scatter | solution.py:157
  571.0 90.6 %copy-start.3 = (bf16[512,2048]{1,0:T(8,128)(2,1)S(1)}, bf16[512,2048]{1,0:T(8,128)(2,1)}, u32[]{:S(2)}) copy-start(bf16[512,2048]{1,0:T(8,128)(2,1)} %all-gather.5.cloned.1.call-done) | copy-start | bytes 6291460
  757.0 10.6 %copy-start.13 = (f32[512,2752]{0,1:T(8,128)S(1)}, f32[512,2752]{0,1:T(8,128)}, u32[]{:S(2)}) copy-start(f32[512,2752]{0,1:T(8,128)} %fusion.47) | copy-start | bytes 16908292
  757.0 10.6 %copy-start.22 = (bf16[128,2752]{0,1:T(8,128)(2,1)S(1)}, bf16[128,2752]{0,1:T(8,128)(2,1)}, u32[]{:S(2)}) copy-start(bf16[128,2752]{0,1:T(8,128)(2,1)} %param.33) | copy-start | bytes 2113540
  757.0 10.6 %copy-start.24 = (f32[512,2752]{0,1:T(8,128)S(1)}, f32[512,2752]{0,1:T(8,128)}, u32[]{:S(2)}) copy-start(f32[512,2752]{0,1:T(8,128)} %fusion.69) | copy-start | bytes 16908292
  757.0 16.1 %slice-start = ((s8[5636096]{0:T(1024)(128)(4,1)}), s8[4194304]{0:T(1024)(128)(4,1)S(1)}, s32[]{:S(2)}) async-start(s8[5636096]{0:T(1024)(128)(4,1)} %bitcast.75), calls=%async_computation.10 | async-start | bytes 8388608
  767.6 4.5 copy-start.14
  767.6 5.5 slice-start.1
  772.1 6.8 copy-start.1
  772.1 4.6 copy-start.25
  778.9 2.5 copy-start.2
  783.0 114.3 %copy-start.4 = (f32[256,2048]{1,0:T(8,128)S(1)}, f32[256,2048]{1,0:T(8,128)}, u32[]{:S(2)}) copy-start(f32[256,2048]{1,0:T(8,128)} %reduce-scatter.4.cloned.1.call-done) | copy-start | bytes 6291460
  783.0 114.3 %copy-start.16 = (bf16[128,2048]{1,0:T(8,128)(2,1)S(1)}, bf16[128,2048]{1,0:T(8,128)(2,1)}, u32[]{:S(2)}) copy-start(bf16[128,2048]{1,0:T(8,128)(2,1)} %param.35) | copy-start | bytes 1572868
  783.0 114.3 %reduce-scatter.6.cloned.1.call-start = ((), (), s32[]{:S(2)}) async-start(), calls=%async_computation.8 | async-start | bytes 3145728 | tf_op jit(solution)/shard_map/reduce_scatter | solution.py:154
Sparse Core Ops, SparseCore 0:
  469.3 56.4 reduce-scatter.3
  530.9 33.0 all-gather.4
  566.2 95.2 all-gather.6
  663.5 93.4 all-gather.8
  759.0 93.4 all-gather.10
  854.5 8.5 reduce-scatter.7
  865.9 31.3 reduce-scatter.5
where the time goes:
time: 908 us; the launch traced here: 907 us
  waiting for transfers between devices  628 us (69%)
  matrix products  136 us (15%)
  starting transfers between devices  60.8 us (7%)
  local copies, waits for them, and re-layouts  44.6 us (5%)
  other arithmetic  23.5 us (3%)
  between operations  13.9 us (2%)
    ppermute x4, waiting for transfers between devices, from_behind(): lax.ppermute(value, axis, [(source, source + steps) for source in range(i...  269 us
    all_gather x1, waiting for transfers between devices, on_device(): lax.all_gather(up_weight, 'seq', axis=0, tiled=True)  85.1 us
    all_gather x1, waiting for transfers between devices, on_device(): lax.all_gather(gate_weight, 'seq', axis=0, tiled=True)  83.8 us
    all_gather x1, waiting for transfers between devices, on_device(): lax.all_gather(down_weight, 'seq', axis=1, tiled=True)  69.4 us
    ppermute x4, starting transfers between devices, from_behind(): lax.ppermute(value, axis, [(source, source + steps) for source in range(i...  60.5 us
    reduce_scatter x1, waiting for transfers between devices, on_device(): lax.psum_scatter(jnp.dot(attended, out_weight, preferred_element_type=jnp...  56.5 us
    dot_general x8, matrix products, one_head(): jnp.einsum('qd,kd->qk', query_one, key_one, preferred_element_type=jnp.fl...  45.9 us
    reduce_scatter x1, waiting for transfers between devices, on_device(): lax.psum_scatter(downward_adapter_term.astype(jnp.bfloat16), 'tp', scatte...  31.5 us
  transfers between devices with their start and end apart: 11, of which 10 were waited for; matrix products, arithmetic and copies ran while one was open for 7% of the time, Pallas kernels for 0%

commit v1 on v0

--- a/solution.py
+++ b/solution.py
@@ -147,7 +147,7 @@
     )
     downward_adapter_term = jnp.dot(
         mixture,
-        lax.all_gather(down_weight, "seq", axis=1, tiled=True),
+        jnp.concatenate(lax.all_gather(down_weight, "seq"), axis=1),
         preferred_element_type=jnp.float32,
     )
     downward_token_rows, rank_rows = (

time: 908 us -> 876 us (0.965)
  waiting for transfers between devices: 628 us -> 582 us
  local copies, waits for them, and re-layouts: 44.6 us -> 56.6 us
    all_gather x1, waiting for transfers between devices: 69.4 us -> 34.2 us  [on_device(): lax.all_gather(down_weight, 'seq')]
    all_gather x0 -> x1, local copies, waits for them, and re-layouts: none -> 15.2 us  [on_device(): lax.all_gather(down_weight, 'seq')]
    all_gather x1, waiting for transfers between devices: 31.3 us -> 17.4 us  [on_device(): normed = lax.all_gather(normed_own, 'tp', axis=0, tiled=True)]
    unnamed x63 -> x61, local copies, waits for them, and re-layouts: 29.1 us -> 25.8 us
  transfers between devices with their start and end apart: 11 -> 11, of which waited for: 10 -> 10; matrix products, arithmetic and copies ran while one was open for 7% -> 6% of each run, Pallas kernels for 0% -> 0%
where the time goes in v1:
time: 876 us; the launch traced here: 874 us
  waiting for transfers between devices  582 us (66%)
  matrix products  136 us (16%)
  starting transfers between devices  60.8 us (7%)
  local copies, waits for them, and re-layouts  56.6 us (6%)
  other arithmetic  23.4 us (3%)
  between operations  15.2 us (2%)
    ppermute x4, waiting for transfers between devices, from_behind(): lax.ppermute(value, axis, [(source, source + steps) for source in range(i...  269 us
    all_gather x1, waiting for transfers between devices, on_device(): lax.all_gather(gate_weight, 'seq', axis=0, tiled=True)  88 us
    all_gather x1, waiting for transfers between devices, on_device(): lax.all_gather(up_weight, 'seq', axis=0, tiled=True)  85 us
    ppermute x4, starting transfers between devices, from_behind(): lax.ppermute(value, axis, [(source, source + steps) for source in range(i...  60.5 us
    reduce_scatter x1, waiting for transfers between devices, on_device(): lax.psum_scatter(jnp.dot(attended, out_weight, preferred_element_type=jnp...  56 us
    dot_general x8, matrix products, one_head(): jnp.einsum('qd,kd->qk', query_one, key_one, preferred_element_type=jnp.fl...  45.9 us
    all_gather x1, waiting for transfers between devices, on_device(): lax.all_gather(down_weight, 'seq')  34.2 us
    reduce_scatter x1, waiting for transfers between devices, on_device(): lax.psum_scatter(downward_adapter_term.astype(jnp.bfloat16), 'tp', scatte...  30.2 us
  transfers between devices with their start and end apart: 11, of which 10 were waited for; matrix products, arithmetic and copies ran while one was open for 6% of the time, Pallas kernels for 0%

profile of v1, /device:TPU:0, one launch (start us, length us, event | category | flops | bytes accessed | tf_op | source)
XLA Modules:
  0.0 874.2 jit_solution(15292636381879094572)
XLA Ops:
  7.4 1.6 copy.28
  9.0 1.9 copy.29
  12.0 2.5 collective-permute-start
  14.6 3.6 collective-permute-done
  18.2 23.8 %collective-permute-start.1 = (bf16[2,512,1024]{1,2,0:T(8,128)(2,1)S(1)}, bf16[2,512,1024]{1,2,0:T(8,128)(2,1)S(1)}, u32[]{:S(2)}, u32[]{:S(2)}) collective-permute-start(bf16[2,512,1024]{1,2,0:T(8,128)(2,1)S(1)} %collective-permute-done), channel_id=1, source_target_pairs={{0,2},{2,4},{4,6},{6,8},{8,10},{10,12},{12,14},{14,16},{16,18},{18... | collective-permute-start | bytes 6291464 | tf_op jit(solution)/shard_map/ppermute | solution.py:19
  42.0 3.6 collective-permute-done.1
  46.3 26.3 %collective-permute-start.2 = (bf16[2,1024,1024]{1,2,0:T(8,128)(2,1)S(1)}, bf16[2,1024,1024]{1,2,0:T(8,128)(2,1)S(1)}, u32[]{:S(2)}, u32[]{:S(2)}) collective-permute-start(bf16[2,1024,1024]{1,2,0:T(8,128)(2,1)S(1)} %pad_maximum_fusion.1), channel_id=1, source_target_pairs={{0,4},{2,6},{4,8},{6,10},{8,12},{10,14},{12,16},{14,18},{16,20},{1... | collective-permute-start | bytes 12582920 | tf_op jit(solution)/shard_map/ppermute | solution.py:19
  72.7 89.8 %collective-permute-done.2 = bf16[2,1024,1024]{1,2,0:T(8,128)(2,1)S(1)} collective-permute-done((bf16[2,1024,1024]{1,2,0:T(8,128)(2,1)S(1)}, bf16[2,1024,1024]{1,2,0:T(8,128)(2,1)S(1)}, u32[]{:S(2)}, u32[]{:S(2)}) %collective-permute-start.2) | collective-permute-done | bytes 4194336 | tf_op jit(solution)/shard_map/ppermute | solution.py:19
  162.5 4.5 pad_maximum_fusion
  167.0 7.8 collective-permute-start.3
  174.8 2.3 copy.27
  177.5 172.0 %collective-permute-done.3 = bf16[2,2048,1024]{1,2,0:T(8,128)(2,1)} collective-permute-done((bf16[2,2048,1024]{1,2,0:T(8,128)(2,1)}, bf16[2,2048,1024]{1,2,0:T(8,128)(2,1)}, u32[]{:S(2)}, u32[]{:S(2)}) %collective-permute-start.3) | collective-permute-done | bytes 8388640 | tf_op jit(solution)/shard_map/ppermute | solution.py:19
  349.5 8.3 constant_dynamic-update-slice_fusion.5
  357.9 4.8 constant_dynamic-update-slice_fusion.4
  362.7 1.5 constant_dynamic-update-slice_fusion.3
  364.2 1.5 constant_dynamic-update-slice_fusion.2
  365.7 1.5 constant_dynamic-update-slice_fusion.1
  367.2 14.5 %fusion.66 = (bf16[1,4608,1024]{1,2,0:T(8,128)(2,1)}, bf16[1,4608,1024]{1,2,0:T(8,128)(2,1)}) fusion(bf16[2,4608,1024]{1,2,0:T(8,128)(2,1)} %constant_dynamic-update-slice_fusion.1), kind=kLoop, calls=%fused_computation.92 | loop fusion | bytes 37748736 | tf_op jit(solution)/shard_map/slice | solution.py:73
  381.7 81.6 %while.11 = (s32[]{:T(128)}, bf16[8,512,128]{1,2,0:T(8,128)(2,1)S(1)}, bf16[8,512,128]{1,2,0:T(8,128)(2,1)}, bf16[8,4608,128]{1,2,0:T(8,128)(2,1)}, bf16[8,4608,...) while((s32[]{:T(128)}, ...), condition=%wide.region_6.7_spmd.clone, body=%wide.region_3.6_spmd.clone.sunk | while | flops 1243413504 | bytes 31514736 | solution.py:89
  381.7 5.7 fusion.97
  387.4 1.4 fusion.98
  388.8 2.9 fusion.99
  391.9 5.7 fusion.97
  397.6 1.4 fusion.98
  399.0 2.9 fusion.99
  402.0 5.7 fusion.97
  407.8 1.4 fusion.98
  409.2 2.9 fusion.99
  412.2 5.7 fusion.97
  418.0 1.4 fusion.98
  419.4 2.9 fusion.99
  422.4 5.7 fusion.97
  428.1 1.4 fusion.98
  429.5 2.9 fusion.99
  432.6 5.7 fusion.97
  438.3 1.4 fusion.98
  439.7 2.9 fusion.99
  442.8 5.7 fusion.97
  448.5 1.4 fusion.98
  449.9 2.9 fusion.99
  452.9 5.7 fusion.97
  458.7 1.4 fusion.98
  460.1 2.9 fusion.99
  463.3 6.6 fusion.68
  470.6 56.0 %reduce-scatter.4.cloned.1.call-done = f32[256,2048]{1,0:T(8,128)} async-done(((f32[512,2048]{1,0:T(8,128)}), f32[256,2048]{1,0:T(8,128)}) %reduce-scatter.4.cloned.1.call-update) | async-done | bytes 2097168 | tf_op jit(solution)/shard_map/reduce_scatter | solution.py:91
  526.6 1.9 multiply_reduce_fusion
  528.6 2.9 multiply_convert_fusion
  532.9 34.2 %all-gather.12.cloned.1.call-done = bf16[44032,128]{1,0:T(8,128)(2,1)} async-done(((bf16[2752,128]{1,0:T(8,128)(2,1)}), bf16[44032,128]{1,0:T(8,128)(2,1)}) %all-gather.12.cloned.1.call-update) | async-done | bytes 11272208 | tf_op jit(solution)/shard_map/all_gather | solution.py:150
  567.1 15.2 %copy.34 = bf16[16,2752,128]{1,2,0:T(8,128)(2,1)} copy(bf16[16,2752,128]{2,1,0:T(8,128)(2,1)} %bitcast.74) | data formatting | bytes 22544384 | tf_op jit(solution)/shard_map/all_gather | solution.py:150
  582.3 17.4 %all-gather.6.cloned.1.call-done = bf16[512,2048]{1,0:T(8,128)(2,1)} async-done(((bf16[256,2048]{1,0:T(8,128)(2,1)}), bf16[512,2048]{1,0:T(8,128)(2,1)}) %all-gather.6.cloned.1.call-update) | async-done | bytes 2097168 | tf_op jit(solution)/shard_map/all_gather | solution.py:102
  599.7 2.3 convolution_convert_fusion.2
  602.1 3.4 fusion.48
  605.5 3.4 fusion.47
  608.9 88.0 %all-gather.8.cloned.1.call-done = bf16[2048,2752]{0,1:T(8,128)(2,1)} async-done(((bf16[128,2752]{0,1:T(8,128)(2,1)}), bf16[2048,2752]{0,1:T(8,128)(2,1)}) %all-gather.8.cloned.1.call-update) | async-done | bytes 11272208 | tf_op jit(solution)/shard_map/all_gather | solution.py:115
  696.8 10.4 %fusion.69 = f32[512,2752]{0,1:T(8,128)} fusion(bf16[512,2048]{1,0:T(8,128)(2,1)S(1)} %copy-done.1, bf16[2048,2752]{0,1:T(8,128)(2,1)} %all-gather.8.cloned.1.call-done), kind=kOutput, calls=%fused_computation.95 | convolution fusion | flops 5771362304 | bytes 19005440 | tf_op jit(solution)/shard_map/dot_general | solution.py:113
  707.2 85.0 %all-gather.10.cloned.1.call-done = bf16[2048,2752]{0,1:T(8,128)(2,1)} async-done(((bf16[128,2752]{0,1:T(8,128)(2,1)}), bf16[2048,2752]{0,1:T(8,128)(2,1)}) %all-gather.10.cloned.1.call-update) | async-done | bytes 11272208 | tf_op jit(solution)/shard_map/all_gather | solution.py:120
  792.3 9.1 %fusion.70 = f32[512,2752]{0,1:T(8,128)S(1)} fusion(bf16[512,2048]{1,0:T(8,128)(2,1)S(1)} %copy-done.1, bf16[2048,2752]{0,1:T(8,128)(2,1)} %all-gather.10.cloned.1.call-done), kind=kOutput, calls=%fused_computation.96 | convolution fusion | flops 5771362304 | bytes 19005440 | tf_op jit(solution)/shard_map/dot_general | solution.py:118
  802.2 2.1 copy-done.24
  804.3 4.7 add_multiply_fusion
  809.1 6.6 add_multiply_fusion.1
  818.2 1.6 fusion.44
  820.0 13.6 %convolution_convert_fusion = bf16[512,2048]{1,0:T(8,128)(2,1)} fusion(bf16[2752,2048]{0,1:T(8,128)(2,1)} %bitcast.73, f32[512,2752]{0,1:T(8,128)} %copy-done.6, f32[512,2752]{0,1:T(8,128)} %copy-done.7, f32[512]{0:T(512)S(1)} %get-tuple-element.111, f32[512]{0:T(512)S(1)} %get-tuple-element.112), kind=kOutput, calls=%fused_computation.26 | convolution fusion | flops 5778046976 | bytes 24645632 | tf_op jit(solution)/shard_map/dot_general | solution.py:148
  833.6 30.2 %reduce-scatter.6.cloned.1.call-done = bf16[256,2048]{1,0:T(8,128)(2,1)} async-done(((bf16[512,2048]{1,0:T(8,128)(2,1)}), bf16[256,2048]{1,0:T(8,128)(2,1)}) %reduce-scatter.6.cloned.1.call-update) | async-done | bytes 1048592 | tf_op jit(solution)/shard_map/reduce_scatter | solution.py:154
  863.8 3.1 fusion.28
  (101 shorter events, 8.6 us)
Async XLA Ops:
  7.4 594.7 %copy-start = (bf16[128,2752]{0,1:T(8,128)(2,1)S(1)}, bf16[128,2752]{0,1:T(8,128)(2,1)}, u32[]{:S(2)}) copy-start(bf16[128,2752]{0,1:T(8,128)(2,1)} %param.32) | copy-start | bytes 2113540
  7.4 519.2 %reduce-scatter.4.cloned.1.call-start = ((), (), s32[]{:S(2)}) async-start(), calls=%async_computation.3 | async-start | bytes 6291456 | tf_op jit(solution)/shard_map/reduce_scatter | solution.py:91
  8.9 1.9 copy-start.9
  10.8 1.0 copy-start.11
  12.0 6.2 collective-permute-start
  18.2 27.5 %collective-permute-start.1 = (bf16[2,512,1024]{1,2,0:T(8,128)(2,1)S(1)}, bf16[2,512,1024]{1,2,0:T(8,128)(2,1)S(1)}, u32[]{:S(2)}, u32[]{:S(2)}) collective-permute-start(bf16[2,512,1024]{1,2,0:T(8,128)(2,1)S(1)} %collective-permute-done), channel_id=1, source_target_pairs={{0,2},{2,4},{4,6},{6,8},{8,10},{10,12},{12,14},{14,16},{16,18},{18... | collective-permute-start | bytes 6291464 | tf_op jit(solution)/shard_map/ppermute | solution.py:19
  45.7 121.3 %copy-start.3 = (bf16[2,512,1024]{1,2,0:T(8,128)(2,1)}, bf16[2,512,1024]{1,2,0:T(8,128)(2,1)S(1)}, u32[]{:S(2)}) copy-start(bf16[2,512,1024]{1,2,0:T(8,128)(2,1)S(1)} %collective-permute-done.1) | copy-start | bytes 6291460
  46.3 130.8 %copy-start.22 = (s32[4]{0:T(128)S(1)}, s32[4]{0:T(128)}, u32[]{:S(2)}) copy-start(s32[4]{0:T(128)} %param.37) | copy-start | bytes 52
  46.3 116.1 %collective-permute-start.2 = (bf16[2,1024,1024]{1,2,0:T(8,128)(2,1)S(1)}, bf16[2,1024,1024]{1,2,0:T(8,128)(2,1)S(1)}, u32[]{:S(2)}, u32[]{:S(2)}) collective-permute-start(bf16[2,1024,1024]{1,2,0:T(8,128)(2,1)S(1)} %pad_maximum_fusion.1), channel_id=1, source_target_pairs={{0,4},{2,6},{4,8},{6,10},{8,12},{10,14},{12,16},{14,18},{16,20},{1... | collective-permute-start | bytes 12582920 | tf_op jit(solution)/shard_map/ppermute | solution.py:19
  162.5 4.5 copy-start.5
  167.0 182.6 %collective-permute-start.3 = (bf16[2,2048,1024]{1,2,0:T(8,128)(2,1)}, bf16[2,2048,1024]{1,2,0:T(8,128)(2,1)}, u32[]{:S(2)}, u32[]{:S(2)}) collective-permute-start(bf16[2,2048,1024]{1,2,0:T(8,128)(2,1)} %pad_maximum_fusion), channel_id=1, source_target_pairs={{0,8},{2,10},{4,12},{6,14},{8,16},{10,18},{12,20},{14,22},{16,24},... | collective-permute-start | bytes 25165832 | tf_op jit(solution)/shard_map/ppermute | solution.py:19
  357.9 4.8 copy-start.4
  362.7 3.0 copy-start.10
  362.7 3.0 copy-start.12
  367.2 14.5 %copy-start.14 = (bf16[8,512,128]{1,2,0:T(8,128)(2,1)S(1)}, bf16[8,512,128]{1,2,0:T(8,128)(2,1)}, u32[]{:S(2)}) copy-start(bf16[8,512,128]{1,2,0:T(8,128)(2,1)} %custom-call.1) | copy-start | bytes 3145732
  463.3 63.3 %copy-start.8 = (bf16[256,2048]{1,0:T(8,128)(2,1)S(1)}, bf16[256,2048]{1,0:T(8,128)(2,1)}, u32[]{:S(2)}) copy-start(bf16[256,2048]{1,0:T(8,128)(2,1)} %param.23) | copy-start | bytes 3145732
  469.9 58.6 %copy-start.19 = (f32[2048]{0:T(1024)S(1)}, f32[2048]{0:T(1024)}, u32[]{:S(2)}) copy-start(f32[2048]{0:T(1024)} %param.25) | copy-start | bytes 24580
  470.0 62.9 %copy-start.20 = (s32[512,2]{0,1:T(2,128)S(1)}, s32[512,2]{0,1:T(2,128)}, u32[]{:S(2)}) copy-start(s32[512,2]{0,1:T(2,128)} %param.36) | copy-start | bytes 12292
  470.0 97.1 %all-gather.12.cloned.1.call-start = ((), (), s32[]{:S(2)}) async-start(), calls=%async_computation.9 | async-start | bytes 11976704 | tf_op jit(solution)/shard_map/all_gather | solution.py:150
  470.6 129.2 %all-gather.6.cloned.1.call-start = ((), (), s32[]{:S(2)}) async-start(), calls=%async_computation.4 | async-start | bytes 3145728 | tf_op jit(solution)/shard_map/all_gather | solution.py:102
  531.5 165.3 %all-gather.8.cloned.1.call-start = ((), (), s32[]{:S(2)}) async-start(), calls=%async_computation.5 | async-start | bytes 11976704 | tf_op jit(solution)/shard_map/all_gather | solution.py:115
  532.1 260.2 %all-gather.10.cloned.1.call-start = ((), (), s32[]{:S(2)}) async-start(), calls=%async_computation.6 | async-start | bytes 11976704 | tf_op jit(solution)/shard_map/all_gather | solution.py:120
  532.8 300.8 %reduce-scatter.8.cloned.1.call-start = ((), (), s32[]{:S(2)}) async-start(), calls=%async_computation.8 | async-start | bytes 196608 | tf_op jit(solution)/shard_map/reduce_scatter | solution.py:157
  567.1 32.6 %copy-start.16 = (bf16[2048,128]{1,0:T(8,128)(2,1)S(1)}, bf16[2048,128]{1,0:T(8,128)(2,1)}, u32[]{:S(2)}) copy-start(bf16[2048,128]{1,0:T(8,128)(2,1)} %param.30) | copy-start | bytes 1572868
  602.0 94.8 %copy-start.1 = (bf16[512,2048]{1,0:T(8,128)(2,1)S(1)}, bf16[512,2048]{1,0:T(8,128)(2,1)}, u32[]{:S(2)}) copy-start(bf16[512,2048]{1,0:T(8,128)(2,1)} %all-gather.6.cloned.1.call-done) | copy-start | bytes 6291460
  707.2 94.2 %copy-start.17 = (bf16[2048,128]{1,0:T(8,128)(2,1)S(1)}, bf16[2048,128]{1,0:T(8,128)(2,1)}, u32[]{:S(2)}) copy-start(bf16[2048,128]{1,0:T(8,128)(2,1)} %param.31) | copy-start | bytes 1572868
  792.3 12.0 %copy-start.21 = (bf16[128,2752]{0,1:T(8,128)(2,1)S(1)}, bf16[128,2752]{0,1:T(8,128)(2,1)}, u32[]{:S(2)}) copy-start(bf16[128,2752]{0,1:T(8,128)(2,1)} %param.33) | copy-start | bytes 2113540
  792.3 12.0 %copy-start.23 = (f32[512,2752]{0,1:T(8,128)S(1)}, f32[512,2752]{0,1:T(8,128)}, u32[]{:S(2)}) copy-start(f32[512,2752]{0,1:T(8,128)} %fusion.69) | copy-start | bytes 16908292
  801.4 2.9 copy-start.24
  801.4 7.6 slice-start
  804.3 4.7 slice-start.1
  809.1 9.2 %copy-start.6 = (f32[512,2752]{0,1:T(8,128)}, f32[512,2752]{0,1:T(8,128)S(1)}, u32[]{:S(2)}) copy-start(f32[512,2752]{0,1:T(8,128)S(1)} %add_multiply_fusion) | copy-start | bytes 16908292
  809.1 6.7 copy-start.18
  809.1 7.4 copy-start.13
  815.8 2.5 copy-start.7
  819.9 43.9 %reduce-scatter.6.cloned.1.call-start = ((), (), s32[]{:S(2)}) async-start(), calls=%async_computation.7 | async-start | bytes 3145728 | tf_op jit(solution)/shard_map/reduce_scatter | solution.py:154
  819.9 43.9 %copy-start.2 = (f32[256,2048]{1,0:T(8,128)S(1)}, f32[256,2048]{1,0:T(8,128)}, u32[]{:S(2)}) copy-start(f32[256,2048]{1,0:T(8,128)} %reduce-scatter.4.cloned.1.call-done) | copy-start | bytes 6291460
  819.9 43.9 %copy-start.15 = (bf16[128,2048]{1,0:T(8,128)(2,1)S(1)}, bf16[128,2048]{1,0:T(8,128)(2,1)}, u32[]{:S(2)}) copy-start(bf16[128,2048]{1,0:T(8,128)(2,1)} %param.35) | copy-start | bytes 1572868
Sparse Core Ops, SparseCore 0:
  470.1 56.4 reduce-scatter.3
  820.0 8.5 reduce-scatter.7
  833.7 30.0 reduce-scatter.5
Sparse Core Ops, SparseCore 1:
  472.8 94.3 all-gather.11
  568.5 31.2 all-gather.5
  601.8 95.0 all-gather.7
  699.0 93.2 all-gather.9
